TPU v7x, 32 devices: a whole 2x2x4 slice. The times are simulated.
32 devices in a mesh: prow: 8 (over z, x), pcol: 4 (over y, core).
Axes of the slice: x: 2, y: 2, z: 4, core: 2. Of those that a mesh axis runs over, the one named last changes fastest.
Arguments:
- inverse_pool: float32 [1536, 1536], P('prow', 'pcol'), may hold values from -6 to 6
- panel_one: float32 [1536, 512], P(('prow', 'pcol')), may hold values from -0.1875 to 0.1875
- panel_two: float32 [1536, 512], P(('prow', 'pcol')), may hold values from -0.21875 to 0.21875
- upper_two: float32 [512, 512], replicated, may hold values from -0.25 to 0.25
- lower_one: float32 [512, 512], replicated, as said below
- lower_two: float32 [512, 512], replicated, as said below
- list_one: int32 [9], replicated, may hold values from 0 to 11, as said below
- list_two: int32 [6], replicated, may hold values from 0 to 11, as said below
Outputs:
- first_offdiag: float32 [1536, 512], P(('prow', 'pcol'))
- first_diag: float32 [512, 512], replicated
- second_offdiag: float32 [1536, 512], P(('prow', 'pcol'))
- second_coupling: float32 [512, 512], replicated
- second_diag: float32 [512, 512], replicated
Inputs may be any that keep to these rules, and one draw needn't show every extreme that they name: `list_one`: distinct block numbers, among them 0, 6 and 11. `list_two`: distinct block numbers, each of which is also in list_one, among them 0, 6 and 11. `lower_one`: lower triangular with a diagonal of 1 to 1.5. `lower_two`: lower triangular with a diagonal of 1 to 1.5.
All inputs are finite; a program needn't handle non-finite values.
Results may differ from a plain program's by a relative error of at most 0.000073.
Values sent between devices are 32-bit elements; how exact they have to be, the bound alone decides.
A program may use at most 64 MiB of HBM per device.

v0:
```python
import jax
import jax.numpy as jnp
from jax import lax
from jax.sharding import PartitionSpec as P

BLK = 128


def product(left, right):
    return jnp.dot(left, right, precision=lax.Precision.HIGHEST, preferred_element_type=jnp.float32)


def transposed_product(left, right):
    return lax.dot_general(
        left,
        right,
        (((0,), (0,)), ((), ())),
        precision=lax.Precision.HIGHEST,
        preferred_element_type=jnp.float32,
    )


def live_rows(listing, first_row, count):
    row_ids = first_row + lax.iota(jnp.int32, count)
    blocks = row_ids // BLK
    hits = jnp.any(blocks[:, None] == listing[None, :], axis=1)
    return jnp.where(hits, 1.0, 0.0).astype(jnp.float32)[:, None]


def multiply_ancestors(inverse_tile, masked_span):
    groups = lax.axis_size("prow") // lax.axis_size("pcol")
    columns = lax.axis_size("pcol")
    span_rows = masked_span.shape[0]
    stacked = lax.all_gather(masked_span, "prow", axis=0, tiled=True)
    grouped = stacked.reshape(columns, groups * span_rows, masked_span.shape[1])
    regrouped = lax.all_to_all(grouped, "pcol", split_axis=0, concat_axis=0, tiled=True)
    accumulated = jnp.einsum(
        "rjkm,kjmw->rw",
        inverse_tile.reshape(inverse_tile.shape[0], groups, columns, span_rows),
        regrouped.reshape(columns, groups, span_rows, masked_span.shape[1]),
        precision=lax.Precision.HIGHEST,
        preferred_element_type=jnp.float32,
    )
    return lax.psum_scatter(accumulated, "pcol", scatter_dimension=0, tiled=True)


def local(inverse_pool, panel_one, panel_two, upper_two, lower_one, lower_two, list_one, list_two):
    span_rows = panel_one.shape[0]
    span_index = lax.axis_index("prow") * lax.axis_size("pcol") + lax.axis_index("pcol")
    first_row = span_index * span_rows
    live_one = live_rows(list_one, first_row, span_rows)
    live_two = live_rows(list_two, first_row, span_rows)
    masked_one = live_one * panel_one
    masked_two = live_two * panel_two
    first_offdiag = -live_one * multiply_ancestors(inverse_pool, masked_one)
    first_terms, coupling_terms = lax.psum(
        (
            transposed_product(masked_one, first_offdiag),
            transposed_product(first_offdiag, masked_two),
        ),
        ("prow", "pcol"),
    )
    second_product = multiply_ancestors(inverse_pool, masked_two)
    second_offdiag = -live_two * (product(first_offdiag, upper_two) + second_product)
    last_terms = lax.psum(transposed_product(masked_two, second_offdiag), ("prow", "pcol"))
    first_diag = transposed_product(lower_one, lower_one) - first_terms
    second_coupling = -(product(first_diag, upper_two) + coupling_terms)
    second_diag = (
        transposed_product(lower_two, lower_two)
        - transposed_product(upper_two, second_coupling)
        - last_terms
    )
    return (first_offdiag, first_diag, second_offdiag, second_coupling, second_diag)


def solution(mesh):
    return jax.shard_map(
        local,
        mesh=mesh,
        in_specs=(
            P("prow", "pcol"),
            P(("prow", "pcol"), None),
            P(("prow", "pcol"), None),
            P(),
            P(),
            P(),
            P(),
            P(),
        ),
        out_specs=(P(("prow", "pcol"), None), P(), P(("prow", "pcol"), None), P(), P()),
        check_vma=False,
    )
```

profile of v0, /device:TPU:0, one launch (start us, length us, event | category | flops | bytes accessed | tf_op | source)
XLA Modules:
  0.0 291.4 jit_solution(14642631012527775425)
XLA Ops:
  7.2 0.7 copy-done.10
  8.0 1.0 broadcast_multiply_fusion.1
  9.0 35.9 %all_gather.6 = f32[384,512]{1,0:T(8,128)} all-gather(f32[48,512]{1,0:T(8,128)S(1)} %broadcast_multiply_fusion.1), channel_id=1, replica_groups=mesh['prow'=8,'pcol'=4] {'prow'}, dimensions={0}, use_global_device_ids=true | all-gather | bytes 884736 | tf_op jit(solution)/shard_map/all_gather | solution.py:34
  44.9 3.6 %all-to-all-start = ((f32[4,96,512]{2,1,0:T(8,128)}), f32[4,96,512]{2,1,0:T(8,128)S(1)}, u32[]{:S(2)}, u32[]{:S(2)}) async-start(f32[4,96,512]{2,1,0:T(8,128)} %bitcast), calls=%async_computation | async-start | bytes 1572864 | tf_op jit(solution)/shard_map/all_to_all | solution.py:36
  48.6 0.2 copy.20
  48.8 0.4 copy-done.11
  49.5 10.6 %all-to-all-done = f32[4,96,512]{2,1,0:T(8,128)S(1)} async-done(((f32[4,96,512]{2,1,0:T(8,128)}), f32[4,96,512]{2,1,0:T(8,128)S(1)}, u32[]{:S(2)}, u32[]{:S(2)}) %all-to-all-start) | async-done | bytes 786464 | tf_op jit(solution)/shard_map/all_to_all | solution.py:36
  60.1 1.6 convolution_bitcast_fusion.2
  61.8 32.3 %all_gather.7 = f32[384,512]{1,0:T(8,128)S(1)} all-gather(f32[48,512]{1,0:T(8,128)S(1)} %broadcast_multiply_fusion), channel_id=1, replica_groups=mesh['prow'=8,'pcol'=4] {'prow'}, dimensions={0}, use_global_device_ids=true | all-gather | bytes 884736 | tf_op jit(solution)/shard_map/all_gather | solution.py:34
  94.1 14.0 %all_to_all.10 = f32[4,96,512]{2,1,0:T(8,128)S(1)} all-to-all(f32[4,96,512]{2,1,0:T(8,128)S(1)} %bitcast.45), channel_id=1, replica_groups=mesh['prow'=8,'pcol'=4] {'pcol'}, dimensions={0} | all-to-all | bytes 1572864 | tf_op jit(solution)/shard_map/all_to_all | solution.py:36
  108.2 1.6 convolution_bitcast_fusion.1
  109.8 0.2 all-reduce.3.cloned.1.call-start
  110.1 1.0 broadcast_multiply_fusion.2
  111.0 2.0 fusion.8
  113.0 2.0 fusion.9
  115.0 15.5 %reduce-scatter.5.cloned.1.call-done = f32[48,512]{1,0:T(8,128)} async-done(((f32[192,512]{1,0:T(8,128)}), f32[48,512]{1,0:T(8,128)}) %reduce-scatter.5.cloned.1.call-update) | async-done | bytes 98320 | tf_op jit(solution)/shard_map/reduce_scatter | solution.py:44
  130.6 1.6 fusion.3
  132.2 2.0 fusion.11
  134.3 1.2 copy-done.1
  135.5 1.9 fusion.10
  137.3 138.8 %all-reduce.3.cloned.1.call-done = (f32[512,512]{1,0:T(8,128)}, f32[512,512]{1,0:T(8,128)}, f32[512,512]{1,0:T(8,128)}) async-done(((f32[512,512]{1,0:T(8,128)}, f32[512,512]{1,0:T(8,128)}, f32[512,512]{1,0:T(8,128)}), (f32[512,512]{1,0:T(8,128)}, f32[512,512]{1,0:T(8,128)}, f32[512,512]{1,0:T(8,128)})) %all-reduce.3.cloned.1.call-update) | async-done | bytes 3145744 | tf_op jit(solution)/shard_map/psum | solution.py:56
  276.2 3.8 %convolution_subtract_fusion = f32[512,512]{1,0:T(8,128)S(1)} fusion(f32[512,512]{1,0:T(8,128)} %get-tuple-element.5, f32[512,512]{1,0:T(8,128)} %param.12), kind=kOutput, calls=%fused_computation.5 | convolution fusion | flops 1610874880 | bytes 3145728 | tf_op jit(solution)/shard_map/dot_general | solution.py:14
  280.0 1.9 fusion.2
  282.0 2.9 fusion.1
  (33 shorter events, 0.6 us)
Async XLA Ops:
  7.2 123.4 %copy-start = (f32[512,512]{1,0:T(8,128)S(1)}, f32[512,512]{1,0:T(8,128)}, u32[]{:S(2)}) copy-start(f32[512,512]{1,0:T(8,128)} %param.11) | copy-start | bytes 3145732
  7.2 0.7 copy-start.10
  44.9 3.7 %copy-start.8 = (f32[192,384]{1,0:T(8,128)S(1)}, f32[192,384]{1,0:T(8,128)}, u32[]{:S(2)}) copy-start(f32[192,384]{1,0:T(8,128)} %param.8) | copy-start | bytes 884740
  44.9 15.2 %all-to-all-start = ((f32[4,96,512]{2,1,0:T(8,128)}), f32[4,96,512]{2,1,0:T(8,128)S(1)}, u32[]{:S(2)}, u32[]{:S(2)}) async-start(f32[4,96,512]{2,1,0:T(8,128)} %bitcast), calls=%async_computation | async-start | bytes 1572864 | tf_op jit(solution)/shard_map/all_to_all | solution.py:36
  48.5 0.7 copy-start.11
  48.6 0.9 copy-start.9
  48.6 61.5 %reduce-scatter.3.cloned.1.call-start = ((), (), s32[]{:S(2)}) async-start(), calls=%async_computation.4 | async-start | bytes 491520 | tf_op jit(solution)/shard_map/reduce_scatter | solution.py:44
  61.8 68.8 %reduce-scatter.5.cloned.1.call-start = ((), (), s32[]{:S(2)}) async-start(), calls=%async_computation.5 | async-start | bytes 491520 | tf_op jit(solution)/shard_map/reduce_scatter | solution.py:44
  109.8 166.4 %all-reduce.3.cloned.1.call-start = ((), (), s32[]{:S(2)}) async-start(), calls=%async_computation.6 | async-start | bytes 6291456 | tf_op jit(solution)/shard_map/psum | solution.py:56
  111.0 19.6 %copy-start.4 = (f32[48,512]{1,0:T(8,128)}, f32[48,512]{1,0:T(8,128)S(1)}, u32[]{:S(2)}) copy-start(f32[48,512]{1,0:T(8,128)S(1)} %broadcast_multiply_fusion.2) | copy-start | bytes 294916
  132.2 2.0 copy-start.7
  134.2 1.2 copy-start.1
  276.2 3.8 %copy-start.6 = (f32[512,512]{1,0:T(8,128)S(1)}, f32[512,512]{1,0:T(8,128)}, u32[]{:S(2)}) copy-start(f32[512,512]{1,0:T(8,128)} %get-tuple-element.6) | copy-start | bytes 3145732
  280.0 2.0 copy-start.3
  280.0 2.0 copy-start.5
  282.0 2.9 copy-start.2
Sparse Core Ops, SparseCore 0:
  61.9 20.7 reduce-scatter.2
  109.9 20.6 reduce-scatter.4
  137.0 139.1 all-reduce.2
where the time goes:
time: 292 us; the launch traced here: 291 us
  waiting for transfers between devices  165 us (57%)
  blocking collectives  82.2 us (28%)
  matrix products  21.3 us (7%)
  between operations  13.9 us (5%)
  starting transfers between devices  3.93 us (1%)
    psum x1, waiting for transfers between devices, local(): lax.psum((transposed_product(masked_one, first_offdiag), transposed_produ...  139 us
    all_gather x2, blocking collectives, multiply_ancestors(): stacked = lax.all_gather(masked_span, 'prow', axis=0, tiled=True)  68.2 us
    reduce_scatter x2, waiting for transfers between devices, multiply_ancestors(): lax.psum_scatter(accumulated, 'pcol', scatter_dimension=0, tiled=True)  15.6 us
    dot_general x6, matrix products, transposed_product(): lax.dot_general(left, right, (((0,), (0,)), ((), ())), precision=lax.Prec...  14.5 us
    all_to_all x1, blocking collectives, multiply_ancestors(): lax.all_to_all(grouped, 'pcol', split_axis=0, concat_axis=0, tiled=True)  14 us
    all_to_all x1, waiting for transfers between devices, multiply_ancestors(): lax.all_to_all(grouped, 'pcol', split_axis=0, concat_axis=0, tiled=True)  10.6 us
  transfers between devices with their start and end apart: 4, of which 3 were waited for; matrix products, arithmetic and copies ran while one was open for 3% of the time, Pallas kernels for 0%

commit v1 on v0

--- a/solution.py
+++ b/solution.py
@@ -54,11 +54,14 @@
     masked_two = live_two * panel_two
     first_offdiag = -live_one * multiply_ancestors(inverse_pool, masked_one)
     first_terms, coupling_terms = lax.psum(
-        (
-            transposed_product(masked_one, first_offdiag),
-            transposed_product(first_offdiag, masked_two),
+        lax.psum(
+            (
+                transposed_product(masked_one, first_offdiag),
+                transposed_product(first_offdiag, masked_two),
+            ),
+            "pcol",
         ),
-        ("prow", "pcol"),
+        "prow",
     )
     second_product = multiply_ancestors(inverse_pool, masked_two)
     second_offdiag = -live_two * (product(first_offdiag, upper_two) + second_product)

time: 292 us -> 424 us (1.45)
  waiting for transfers between devices: 165 us -> 287 us
  blocking collectives: 82.2 us -> 90.9 us
    psum x0 -> x2, waiting for transfers between devices: none -> 232 us  [the longest x1 130 us: local(): lax.psum(transposed_product(masked_two, second_offdiag), ('prow', 'pcol'))]
    psum x1, waiting for transfers between devices: 139 us -> 3.17 us  [local(): lax.psum((transposed_product(masked_one, first_offdiag), transposed_produ...]
    reduce_scatter x2, waiting for transfers between devices: 15.6 us -> 40.8 us  [multiply_ancestors(): lax.psum_scatter(accumulated, 'pcol', scatter_dimension=0, tiled=True)]
    all_to_all x1, blocking collectives: 14 us -> 22.9 us  [multiply_ancestors(): lax.all_to_all(grouped, 'pcol', split_axis=0, concat_axis=0, tiled=True)]
  transfers between devices with their start and end apart: 4 -> 6, of which waited for: 3 -> 6; matrix products, arithmetic and copies ran while one was open for 3% -> 3% of each run, Pallas kernels for 0% -> 0%
where the time goes in v1:
time: 424 us
  waiting for transfers between devices  287 us (68%)
  blocking collectives  90.9 us (21%)
  matrix products  21.8 us (5%)
  between operations  13.9 us (3%)
    psum x1, waiting for transfers between devices, local(): lax.psum(transposed_product(masked_two, second_offdiag), ('prow', 'pcol'))  130 us
    psum x1, waiting for transfers between devices, local(): lax.psum(lax.psum((transposed_product(masked_one, first_offdiag), transpo...  102 us
    all_gather x2, blocking collectives, multiply_ancestors(): stacked = lax.all_gather(masked_span, 'prow', axis=0, tiled=True)  68.1 us
    reduce_scatter x2, waiting for transfers between devices, multiply_ancestors(): lax.psum_scatter(accumulated, 'pcol', scatter_dimension=0, tiled=True)  40.8 us
    all_to_all x1, blocking collectives, multiply_ancestors(): lax.all_to_all(grouped, 'pcol', split_axis=0, concat_axis=0, tiled=True)  22.9 us
    dot_general x6, matrix products, transposed_product(): lax.dot_general(left, right, (((0,), (0,)), ((), ())), precision=lax.Prec...  15.1 us
    all_to_all x1, waiting for transfers between devices, multiply_ancestors(): lax.all_to_all(grouped, 'pcol', split_axis=0, concat_axis=0, tiled=True)  11.4 us
  transfers between devices with their start and end apart: 6, of which 6 were waited for; matrix products, arithmetic and copies ran while one was open for 3% of the time, Pallas kernels for 0%

profile of v1, /device:TPU:0, one launch (start us, length us, event | category | flops | bytes accessed | tf_op | source)
XLA Modules:
  0.0 423.7 jit_solution(12090346021733940570)
XLA Ops:
  8.0 1.0 broadcast_multiply_fusion.1
  9.0 35.9 %all_gather.6 = f32[384,512]{1,0:T(8,128)} all-gather(f32[48,512]{1,0:T(8,128)S(1)} %broadcast_multiply_fusion.1), channel_id=1, replica_groups=mesh['prow'=8,'pcol'=4] {'prow'}, dimensions={0}, use_global_device_ids=true | all-gather | bytes 884736 | tf_op jit(solution)/shard_map/all_gather | solution.py:34
  44.9 3.6 all-to-all-start
  48.8 11.4 %all-to-all-done = f32[4,96,512]{2,1,0:T(8,128)S(1)} async-done(((f32[4,96,512]{2,1,0:T(8,128)}), f32[4,96,512]{2,1,0:T(8,128)S(1)}, u32[]{:S(2)}, u32[]{:S(2)}) %all-to-all-start) | async-done | bytes 786464 | tf_op jit(solution)/shard_map/all_to_all | solution.py:36
  60.1 1.6 convolution_bitcast_fusion.2
  62.7 19.9 %reduce-scatter.3.cloned.1.call-done = f32[48,512]{1,0:T(8,128)} async-done(((f32[192,512]{1,0:T(8,128)}), f32[48,512]{1,0:T(8,128)}) %reduce-scatter.3.cloned.1.call-update) | async-done | bytes 98320 | tf_op jit(solution)/shard_map/reduce_scatter | solution.py:44
  82.7 1.0 broadcast_multiply_fusion.2
  83.6 2.0 fusion.8
  85.7 2.0 fusion.9
  87.7 32.2 %all_gather.7 = f32[384,512]{1,0:T(8,128)S(1)} all-gather(f32[48,512]{1,0:T(8,128)S(1)} %broadcast_multiply_fusion), channel_id=1, replica_groups=mesh['prow'=8,'pcol'=4] {'prow'}, dimensions={0}, use_global_device_ids=true | all-gather | bytes 884736 | tf_op jit(solution)/shard_map/all_gather | solution.py:34
  119.9 22.9 %all_to_all.10 = f32[4,96,512]{2,1,0:T(8,128)S(1)} all-to-all(f32[4,96,512]{2,1,0:T(8,128)S(1)} %bitcast.45), channel_id=1, replica_groups=mesh['prow'=8,'pcol'=4] {'pcol'}, dimensions={0} | all-to-all | bytes 1572864 | tf_op jit(solution)/shard_map/all_to_all | solution.py:36
  142.8 1.6 convolution_bitcast_fusion.1
  144.5 3.2 all-reduce.10.cloned.1.call-done
  147.9 1.0 copy-done.1
  148.9 1.9 fusion.10
  150.7 20.9 %reduce-scatter.5.cloned.1.call-done = f32[48,512]{1,0:T(8,128)} async-done(((f32[192,512]{1,0:T(8,128)}), f32[48,512]{1,0:T(8,128)}) %reduce-scatter.5.cloned.1.call-update) | async-done | bytes 98320 | tf_op jit(solution)/shard_map/reduce_scatter | solution.py:44
  171.6 1.6 fusion.3
  173.3 2.0 fusion.11
  175.3 102.2 %all-reduce.8.cloned.1.call-done = (f32[512,512]{1,0:T(8,128)}, f32[512,512]{1,0:T(8,128)}) async-done(((f32[512,512]{1,0:T(8,128)}, f32[512,512]{1,0:T(8,128)}), (f32[512,512]{1,0:T(8,128)}, f32[512,512]{1,0:T(8,128)})) %all-reduce.8.cloned.1.call-update) | async-done | bytes 2097168 | tf_op jit(solution)/shard_map/psum | solution.py:56
  277.5 3.2 convolution_subtract_fusion
  280.7 1.0 copy-done.4
  281.6 1.8 fusion.2
  283.5 129.6 %all-reduce.6.cloned.1.call-done = f32[512,512]{1,0:T(8,128)} async-done(((f32[512,512]{1,0:T(8,128)}), f32[512,512]{1,0:T(8,128)}) %all-reduce.6.cloned.1.call-update) | async-done | bytes 1048592 | tf_op jit(solution)/shard_map/psum | solution.py:68
  413.1 4.1 fusion.1
  (39 shorter events, 2.4 us)
Async XLA Ops:
  7.2 164.5 %copy-start = (f32[512,512]{1,0:T(8,128)S(1)}, f32[512,512]{1,0:T(8,128)}, u32[]{:S(2)}) copy-start(f32[512,512]{1,0:T(8,128)} %param.11) | copy-start | bytes 3145732
  7.2 0.7 copy-start.10
  44.9 3.7 copy-start.8
  44.9 15.2 %all-to-all-start = ((f32[4,96,512]{2,1,0:T(8,128)}), f32[4,96,512]{2,1,0:T(8,128)S(1)}, u32[]{:S(2)}, u32[]{:S(2)}) async-start(f32[4,96,512]{2,1,0:T(8,128)} %bitcast), calls=%async_computation | async-start | bytes 1572864 | tf_op jit(solution)/shard_map/all_to_all | solution.py:36
  48.5 34.1 %reduce-scatter.3.cloned.1.call-start = ((), (), s32[]{:S(2)}) async-start(), calls=%async_computation.4 | async-start | bytes 491520 | tf_op jit(solution)/shard_map/reduce_scatter | solution.py:44
  61.8 0.7 copy-start.11
  61.8 0.9 copy-start.9
  61.8 85.8 %all-reduce.10.cloned.1.call-start = ((), (), s32[]{:S(2)}) async-start(), calls=%async_computation.8 | async-start | bytes 4194304 | tf_op jit(solution)/shard_map/psum | solution.py:57
  83.6 88.0 %copy-start.5 = (f32[48,512]{1,0:T(8,128)}, f32[48,512]{1,0:T(8,128)S(1)}, u32[]{:S(2)}) copy-start(f32[48,512]{1,0:T(8,128)S(1)} %broadcast_multiply_fusion.2) | copy-start | bytes 294916
  87.7 83.9 %reduce-scatter.5.cloned.1.call-start = ((), (), s32[]{:S(2)}) async-start(), calls=%async_computation.5 | async-start | bytes 491520 | tf_op jit(solution)/shard_map/reduce_scatter | solution.py:44
  144.4 133.0 %all-reduce.8.cloned.1.call-start = ((), (), s32[]{:S(2)}) async-start(), calls=%async_computation.7 | async-start | bytes 4194304 | tf_op jit(solution)/shard_map/psum | solution.py:56
  147.6 1.2 copy-start.1
  147.7 265.4 %all-reduce.6.cloned.1.call-start = ((), (), s32[]{:S(2)}) async-start(), calls=%async_computation.6 | async-start | bytes 2097152 | tf_op jit(solution)/shard_map/psum | solution.py:68
  173.2 2.0 copy-start.7
  173.3 104.2 %copy-start.2 = (f32[512,512]{1,0:T(8,128)S(1)}, f32[512,512]{1,0:T(8,128)}, u32[]{:S(2)}) copy-start(f32[512,512]{1,0:T(8,128)} %param.12) | copy-start | bytes 3145732
  277.5 4.2 copy-start.6
  280.6 1.0 copy-start.4
  283.5 133.7 %copy-start.3 = (f32[512,512]{1,0:T(8,128)}, f32[512,512]{1,0:T(8,128)S(1)}, u32[]{:S(2)}) copy-start(f32[512,512]{1,0:T(8,128)S(1)} %fusion.2) | copy-start | bytes 3145732
Sparse Core Ops, SparseCore 0:
  61.9 20.7 reduce-scatter.2
  87.8 59.7 all-reduce.9
  150.7 20.8 reduce-scatter.4
  175.1 102.2 all-reduce.7
  283.1 129.9 all-reduce.5
